TPU v7x, 256 devices: a whole 4x4x8 slice. The times are simulated.
256 devices in a mesh: section: 8 (over y, x_hi), dp: 32 (over z, x_lo, core).
Axes of the slice: x: 4 (x_hi: 2, x_lo: 2; x = x_hi * 2 + x_lo), y: 4, z: 8, core: 2. Of those that a mesh axis runs over, the one named last changes fastest.
Arguments:
- clips: bfloat16 [64, 14, 8, 640], P('dp'), may hold values from -6 to 6
- cotangent: bfloat16 [64, 14, 8, 640], P('dp'), may hold values from -6 to 6
- timesteps: int32 [64], P('dp'), may hold values from 0 to 999
- time_table: bfloat16 [8, 1000, 640], P('section'), may hold values from -3 to 3
- skip_weights: bfloat16 [8, 640, 640], P('section'), may hold values from -0.125 to 0.125
- conv_weights: bfloat16 [8, 1920, 640], P('section'), may hold values from -0.125 to 0.125
- gains: float32 [8, 640], P('section'), may hold values from 0.5 to 1.5
Outputs:
- grad_skip: float32 [8, 640, 640], P('section')
- grad_conv: float32 [8, 1920, 640], P('section')
- grad_gain: float32 [8, 640], P('section')
All inputs are finite; a program needn't handle non-finite values.
Results may differ from a plain program's by a relative error of at most 0.017.
Values may be sent and summed in bfloat16 or wider, within the bound.
No kernel may reach another device: no remote copies, remote signals or barrier semaphores. Data moves between devices by JAX's collectives and lax.ppermute only.
A program may use at most 64 MiB of HBM per device.

v0:
```python
import jax
import jax.numpy as jnp
from jax import lax
from jax.sharding import PartitionSpec as P

EPSILON = 1e-05


def swapped(value, axis, apart):
    mask = 2**apart
    pairs = [(source, source ^ mask) for source in range(lax.axis_size(axis))]
    return lax.ppermute(value, axis, pairs)


def passed_along(value, axis, steps):
    count = lax.axis_size(axis)
    initial, last = (max(0, -steps), min(count, count - steps))
    return lax.ppermute(value, axis, [(source, source + steps) for source in range(initial, last)])


def stack_taps(normed):
    zero_frame = jnp.zeros_like(normed[..., :1, :, :])
    before = jnp.concatenate([zero_frame, normed[..., :-1, :, :]], axis=-3)
    after = jnp.concatenate([normed[..., 1:, :, :], zero_frame], axis=-3)
    return jnp.concatenate([before, normed, after], axis=-1)


def unstack_taps(tapped):
    width = tapped.shape[-1] // 3
    first_tap = tapped[..., :width]
    middle_tap = tapped[..., width : 2 * width]
    last_tap = tapped[..., 2 * width :]
    zero_frame = jnp.zeros_like(first_tap[..., :1, :, :])
    later = jnp.concatenate([first_tap[..., 1:, :, :], zero_frame], axis=-3)
    earlier = jnp.concatenate([zero_frame, last_tap[..., :-1, :, :]], axis=-3)
    return middle_tap + later + earlier


def right_dot(left, right):
    return lax.dot_general(
        left, right, (((2,), (0,)), ((), ())), preferred_element_type=jnp.float32
    )


def right_dot_transposed(left, right):
    return lax.dot_general(
        left, right, (((2,), (1,)), ((), ())), preferred_element_type=jnp.float32
    )


def outer_sum(left, right):
    return lax.dot_general(
        left, right, (((0, 1), (0, 1)), ((), ())), preferred_element_type=jnp.float32
    )


def forward_level(inbound, skip_in, skip_weight, conv_weight, gain_row, embed):
    mixed = inbound.astype(jnp.float32) + right_dot(skip_in, skip_weight) + embed
    inv_rms = lax.rsqrt(jnp.mean(mixed * mixed, axis=-1, keepdims=True) + EPSILON)
    normed = (mixed * inv_rms * gain_row).astype(jnp.bfloat16)
    conv_out = right_dot(stack_taps(normed), conv_weight)
    output = (mixed + jax.nn.silu(conv_out)).astype(jnp.bfloat16)
    return (output, mixed, normed, conv_out)


def backward_level(upstream, skip_in, mixed, normed, conv_out, skip_weight, conv_weight, gain_row):
    inv_rms = lax.rsqrt(jnp.mean(mixed * mixed, axis=-1, keepdims=True) + EPSILON)
    sigmoid = jax.nn.sigmoid(conv_out)
    conv_grad = (upstream * sigmoid * (1.0 + conv_out * (1.0 - sigmoid))).astype(jnp.bfloat16)
    grad_conv = outer_sum(stack_taps(normed), conv_grad)
    normed_grad = unstack_taps(right_dot_transposed(conv_grad, conv_weight))
    unit = mixed * inv_rms
    grad_gain = jnp.sum(normed_grad * unit, axis=(0, 1))
    scaled = normed_grad * gain_row
    mixed_grad = upstream + inv_rms * (
        scaled - unit * jnp.mean(scaled * unit, axis=-1, keepdims=True)
    )
    mixed_low = mixed_grad.astype(jnp.bfloat16)
    grad_skip = outer_sum(skip_in, mixed_low)
    skip_grad = right_dot_transposed(mixed_low, skip_weight)
    return (mixed_grad, skip_grad, grad_skip, grad_conv, grad_gain)


def local(clips, cotangent, timesteps, time_table, skip_weights, conv_weights, gains):
    level_count = lax.axis_size("section")
    level_index = lax.axis_index("section")
    half_levels = level_count // 2
    encoder = level_index < half_levels
    first_level = level_index == 0
    last_level = level_index == level_count - 1
    skip_weight = skip_weights[0]
    conv_weight = conv_weights[0]
    gain_row = gains[0]
    micro_count = clips.shape[0]
    tick_count = micro_count + level_count - 1
    step_ids = jnp.arange(time_table.shape[1], dtype=jnp.int32)
    one_hot = (timesteps[:, None] == step_ids[None, :]).astype(jnp.bfloat16)
    embeds = jnp.dot(one_hot, time_table[0], preferred_element_type=jnp.float32)

    def mirror(value):
        for bit_index in range(level_count.bit_length() - 1):
            value = swapped(value, "section", bit_index)
        return value

    def in_range(slot):
        return (slot >= 0) & (slot < micro_count)

    def take(buffer, slot):
        return lax.dynamic_index_in_dim(
            buffer, jnp.clip(slot, 0, micro_count - 1), 0, keepdims=False
        )

    def store(buffer, slot, value, active):
        slot_safe = jnp.clip(slot, 0, micro_count - 1)
        kept = lax.dynamic_index_in_dim(buffer, slot_safe, 0, keepdims=False)
        return lax.dynamic_update_index_in_dim(buffer, jnp.where(active, value, kept), slot_safe, 0)

    zeros_low = jnp.zeros(clips.shape, jnp.bfloat16)
    zeros_high = jnp.zeros(clips.shape, jnp.float32)
    frame_zeros = jnp.zeros(clips.shape[1:], jnp.bfloat16)

    def forward_tick(state_carry, tick):
        inbound, skip_slots, saved_skip, saved_mixed, saved_normed, saved_conv = state_carry
        micro = tick - level_index
        active = in_range(micro)
        source = jnp.where(first_level, take(clips, micro), inbound)
        skip_in = jnp.where(encoder, source, take(skip_slots, micro))
        output, mixed, normed, conv_out = forward_level(
            source, skip_in, skip_weight, conv_weight, gain_row, take(embeds, micro)
        )
        saved_skip = store(saved_skip, micro, skip_in, active)
        saved_mixed = store(saved_mixed, micro, mixed, active)
        saved_normed = store(saved_normed, micro, normed, active)
        saved_conv = store(saved_conv, micro, conv_out, active)
        inbound = passed_along(output, "section", 1)
        arrived = mirror(output)
        incoming = tick - (level_count - 1 - level_index)
        skip_slots = store(
            skip_slots, incoming, arrived, in_range(incoming) & jnp.logical_not(encoder)
        )
        return ((inbound, skip_slots, saved_skip, saved_mixed, saved_normed, saved_conv), None)

    forward_state = (frame_zeros, zeros_low, zeros_low, zeros_high, zeros_low, zeros_high)
    forward_state, _ = lax.scan(
        forward_tick, forward_state, jnp.arange(tick_count, dtype=jnp.int32)
    )
    _, _, saved_skip, saved_mixed, saved_normed, saved_conv = forward_state

    def backward_tick(state_carry, tick):
        inbound, grad_slots, total_skip, total_conv, total_gain = state_carry
        micro = tick - (level_count - 1 - level_index)
        active = in_range(micro)
        upstream = jnp.where(last_level, take(cotangent, micro), inbound).astype(jnp.float32)
        upstream = upstream + jnp.where(encoder, take(grad_slots, micro).astype(jnp.float32), 0.0)
        mixed_grad, skip_grad, grad_skip, grad_conv, grad_gain = backward_level(
            upstream,
            take(saved_skip, micro),
            take(saved_mixed, micro),
            take(saved_normed, micro),
            take(saved_conv, micro),
            skip_weight,
            conv_weight,
            gain_row,
        )
        total_skip = total_skip + jnp.where(active, grad_skip, 0.0)
        total_conv = total_conv + jnp.where(active, grad_conv, 0.0)
        total_gain = total_gain + jnp.where(active, grad_gain, 0.0)
        sent_back = jnp.where(encoder, mixed_grad + skip_grad, mixed_grad).astype(jnp.bfloat16)
        inbound = passed_along(sent_back, "section", -1)
        arrived = mirror(skip_grad.astype(jnp.bfloat16))
        incoming = tick - level_index
        grad_slots = store(grad_slots, incoming, arrived, in_range(incoming) & encoder)
        return ((inbound, grad_slots, total_skip, total_conv, total_gain), None)

    backward_state = (
        frame_zeros,
        zeros_low,
        jnp.zeros(skip_weight.shape, jnp.float32),
        jnp.zeros(conv_weight.shape, jnp.float32),
        jnp.zeros(gain_row.shape, jnp.float32),
    )
    backward_state, _ = lax.scan(
        backward_tick, backward_state, jnp.arange(tick_count, dtype=jnp.int32)
    )
    _, _, total_skip, total_conv, total_gain = backward_state
    summed_skip, summed_conv, summed_gain = lax.psum((total_skip, total_conv, total_gain), "dp")
    clip_total = micro_count * lax.axis_size("dp")
    return (
        (summed_skip / clip_total)[None],
        (summed_conv / clip_total)[None],
        (summed_gain / clip_total)[None],
    )


def solution(mesh):
    placed = (
        P("dp", None, None, None),
        P("dp", None, None, None),
        P("dp"),
        P("section", None, None),
        P("section", None, None),
        P("section", None, None),
        P("section", None),
    )
    return jax.shard_map(
        local,
        mesh=mesh,
        in_specs=placed,
        out_specs=(P("section", None, None), P("section", None, None), P("section", None)),
        check_vma=False,
    )
```

profile of v0, /device:TPU:8, one launch (start us, length us, event | category | flops | bytes accessed | tf_op | source)
XLA Modules:
  0.0 890.7 jit_solution(13313965460681185647)
XLA Ops:
  12.5 271.8 %while.41 = (s32[]{:T(128)}, bf16[14,8,640]{2,1,0:T(8,128)(2,1)S(1)}, bf16[2,14,8,640]{3,2,1,0:T(8,128)(2,1)S(1)}, bf16[2,14,8,640]{3,2,1,0:T(8,128)(2,1)}, f32[...) while((s32[]{:T(128)}, ...), condition=%wide.region_2.3_spmd, body=%wide.region_0.2_spmd.sunk | while | flops 370872448 | bytes 14131990 | solution.py:144
  90.1 5.7 collective-permute-done.2
  246.6 5.9 collective-permute-done.3
  276.7 5.8 collective-permute-done.3
  284.9 344.0 %while.42 = (s32[]{:T(128)}, bf16[14,8,640]{2,1,0:T(8,128)(2,1)S(1)}, bf16[2,14,8,640]{3,2,1,0:T(8,128)(2,1)S(1)}, f32[640,640]{1,0:T(8,128)}, f32[1920,640]{1,0...) while((s32[]{:T(128)}, ...), condition=%wide.region_7.8_spmd.clone, body=%wide.region_3.7_spmd.clone.sunk | while | flops 744009088 | bytes 32475900 | solution.py:182
  314.7 6.6 collective-permute-done.7
  340.1 5.6 fusion.96
  353.2 7.0 collective-permute-done.7
  378.9 5.6 fusion.96
  392.7 6.2 collective-permute-done.7
  417.6 5.6 fusion.96
  431.8 6.6 collective-permute-done.7
  457.2 5.6 fusion.96
  469.9 6.6 collective-permute-done.7
  495.2 5.6 fusion.96
  508.0 6.6 collective-permute-done.7
  533.3 5.6 fusion.96
  546.1 6.6 collective-permute-done.7
  571.4 5.6 fusion.96
  584.1 6.6 collective-permute-done.7
  609.5 5.6 fusion.96
  622.2 6.6 collective-permute-done.7
  629.6 53.6 %psum.23 = f32[640]{0:T(1024)S(1)} all-reduce(f32[640]{0:T(1024)S(1)} %copy-done.13), channel_id=1, replica_groups=mesh['section'=8,'dp'=32] {'dp'}, use_global_device_ids=true, to_apply=%region_10.11 | all-reduce | flops 640 | bytes 5120 | tf_op jit(solution)/shard_map/psum | solution.py:186
  683.7 192.5 %all-reduce.9.cloned.1.call-done = (f32[640,640]{1,0:T(8,128)}, f32[1920,640]{1,0:T(8,128)}) async-done(((f32[640,640]{1,0:T(8,128)}, f32[1920,640]{1,0:T(8,128)}), (f32[640,640]{1,0:T(8,128)}, f32[1920,640]{1,0:T(8,128)})) %all-reduce.9.cloned.1.call-update) | async-done | bytes 6553616 | tf_op jit(solution)/shard_map/psum | solution.py:186
  (629 shorter events, 482.9 us)
Async XLA Ops:
  7.2 869.0 %all-reduce.9.cloned.1.call-start = ((), (), s32[]{:S(2)}) async-start(), calls=%async_computation | async-start | bytes 13107200 | tf_op jit(solution)/shard_map/psum | solution.py:186
  23.5 20.6 %collective-permute-start = (bf16[14,8,640]{2,1,0:T(8,128)(2,1)}, bf16[14,8,640]{2,1,0:T(8,128)(2,1)S(1)}, u32[]{:S(2)}, u32[]{:S(2)}) collective-permute-start(bf16[14,8,640]{2,1,0:T(8,128)(2,1)} %get-tuple-element.766), channel_id=1, source_target_pairs={{0,32},{32,64},{64,96},{96,128},{128,160},{160,192},{192,224},{1,3... | collective-permute-start | bytes 430088 | tf_op jit(solution)/shard_map/while/body/eval_jaxpr/ppermute | solution.py:18
  53.6 20.5 %collective-permute-start = (bf16[14,8,640]{2,1,0:T(8,128)(2,1)}, bf16[14,8,640]{2,1,0:T(8,128)(2,1)S(1)}, u32[]{:S(2)}, u32[]{:S(2)}) collective-permute-start(bf16[14,8,640]{2,1,0:T(8,128)(2,1)} %get-tuple-element.766), channel_id=1, source_target_pairs={{0,32},{32,64},{64,96},{96,128},{128,160},{160,192},{192,224},{1,3... | collective-permute-start | bytes 430088 | tf_op jit(solution)/shard_map/while/body/eval_jaxpr/ppermute | solution.py:18
  84.6 19.9 %collective-permute-start = (bf16[14,8,640]{2,1,0:T(8,128)(2,1)}, bf16[14,8,640]{2,1,0:T(8,128)(2,1)S(1)}, u32[]{:S(2)}, u32[]{:S(2)}) collective-permute-start(bf16[14,8,640]{2,1,0:T(8,128)(2,1)} %get-tuple-element.766), channel_id=1, source_target_pairs={{0,32},{32,64},{64,96},{96,128},{128,160},{160,192},{192,224},{1,3... | collective-permute-start | bytes 430088 | tf_op jit(solution)/shard_map/while/body/eval_jaxpr/ppermute | solution.py:18
  113.3 19.9 %collective-permute-start = (bf16[14,8,640]{2,1,0:T(8,128)(2,1)}, bf16[14,8,640]{2,1,0:T(8,128)(2,1)S(1)}, u32[]{:S(2)}, u32[]{:S(2)}) collective-permute-start(bf16[14,8,640]{2,1,0:T(8,128)(2,1)} %get-tuple-element.766), channel_id=1, source_target_pairs={{0,32},{32,64},{64,96},{96,128},{128,160},{160,192},{192,224},{1,3... | collective-permute-start | bytes 430088 | tf_op jit(solution)/shard_map/while/body/eval_jaxpr/ppermute | solution.py:18
  142.0 19.9 %collective-permute-start = (bf16[14,8,640]{2,1,0:T(8,128)(2,1)}, bf16[14,8,640]{2,1,0:T(8,128)(2,1)S(1)}, u32[]{:S(2)}, u32[]{:S(2)}) collective-permute-start(bf16[14,8,640]{2,1,0:T(8,128)(2,1)} %get-tuple-element.766), channel_id=1, source_target_pairs={{0,32},{32,64},{64,96},{96,128},{128,160},{160,192},{192,224},{1,3... | collective-permute-start | bytes 430088 | tf_op jit(solution)/shard_map/while/body/eval_jaxpr/ppermute | solution.py:18
  170.7 19.9 %collective-permute-start = (bf16[14,8,640]{2,1,0:T(8,128)(2,1)}, bf16[14,8,640]{2,1,0:T(8,128)(2,1)S(1)}, u32[]{:S(2)}, u32[]{:S(2)}) collective-permute-start(bf16[14,8,640]{2,1,0:T(8,128)(2,1)} %get-tuple-element.766), channel_id=1, source_target_pairs={{0,32},{32,64},{64,96},{96,128},{128,160},{160,192},{192,224},{1,3... | collective-permute-start | bytes 430088 | tf_op jit(solution)/shard_map/while/body/eval_jaxpr/ppermute | solution.py:18
  199.5 20.9 %collective-permute-start = (bf16[14,8,640]{2,1,0:T(8,128)(2,1)}, bf16[14,8,640]{2,1,0:T(8,128)(2,1)S(1)}, u32[]{:S(2)}, u32[]{:S(2)}) collective-permute-start(bf16[14,8,640]{2,1,0:T(8,128)(2,1)} %get-tuple-element.766), channel_id=1, source_target_pairs={{0,32},{32,64},{64,96},{96,128},{128,160},{160,192},{192,224},{1,3... | collective-permute-start | bytes 430088 | tf_op jit(solution)/shard_map/while/body/eval_jaxpr/ppermute | solution.py:18
  230.2 24.1 %collective-permute-start = (bf16[14,8,640]{2,1,0:T(8,128)(2,1)}, bf16[14,8,640]{2,1,0:T(8,128)(2,1)S(1)}, u32[]{:S(2)}, u32[]{:S(2)}) collective-permute-start(bf16[14,8,640]{2,1,0:T(8,128)(2,1)} %get-tuple-element.766), channel_id=1, source_target_pairs={{0,32},{32,64},{64,96},{96,128},{128,160},{160,192},{192,224},{1,3... | collective-permute-start | bytes 430088 | tf_op jit(solution)/shard_map/while/body/eval_jaxpr/ppermute | solution.py:18
  262.3 21.9 %collective-permute-start = (bf16[14,8,640]{2,1,0:T(8,128)(2,1)}, bf16[14,8,640]{2,1,0:T(8,128)(2,1)S(1)}, u32[]{:S(2)}, u32[]{:S(2)}) collective-permute-start(bf16[14,8,640]{2,1,0:T(8,128)(2,1)} %get-tuple-element.766), channel_id=1, source_target_pairs={{0,32},{32,64},{64,96},{96,128},{128,160},{160,192},{192,224},{1,3... | collective-permute-start | bytes 430088 | tf_op jit(solution)/shard_map/while/body/eval_jaxpr/ppermute | solution.py:18
  296.4 25.0 %collective-permute-start.4 = (bf16[14,8,640]{2,1,0:T(8,128)(2,1)}, bf16[14,8,640]{2,1,0:T(8,128)(2,1)S(1)}, u32[]{:S(2)}, u32[]{:S(2)}) collective-permute-start(bf16[14,8,640]{2,1,0:T(8,128)(2,1)} %get-tuple-element.802), channel_id=1, source_target_pairs={{32,0},{64,32},{96,64},{128,96},{160,128},{192,160},{224,192},{33,... | collective-permute-start | bytes 430088 | tf_op jit(solution)/shard_map/while/body/eval_jaxpr/ppermute | solution.py:18
  332.9 27.3 %collective-permute-start.4 = (bf16[14,8,640]{2,1,0:T(8,128)(2,1)}, bf16[14,8,640]{2,1,0:T(8,128)(2,1)S(1)}, u32[]{:S(2)}, u32[]{:S(2)}) collective-permute-start(bf16[14,8,640]{2,1,0:T(8,128)(2,1)} %get-tuple-element.802), channel_id=1, source_target_pairs={{32,0},{64,32},{96,64},{128,96},{160,128},{192,160},{224,192},{33,... | collective-permute-start | bytes 430088 | tf_op jit(solution)/shard_map/while/body/eval_jaxpr/ppermute | solution.py:18
  371.7 27.1 %collective-permute-start.4 = (bf16[14,8,640]{2,1,0:T(8,128)(2,1)}, bf16[14,8,640]{2,1,0:T(8,128)(2,1)S(1)}, u32[]{:S(2)}, u32[]{:S(2)}) collective-permute-start(bf16[14,8,640]{2,1,0:T(8,128)(2,1)} %get-tuple-element.802), channel_id=1, source_target_pairs={{32,0},{64,32},{96,64},{128,96},{160,128},{192,160},{224,192},{33,... | collective-permute-start | bytes 430088 | tf_op jit(solution)/shard_map/while/body/eval_jaxpr/ppermute | solution.py:18
  410.4 28.1 %collective-permute-start.4 = (bf16[14,8,640]{2,1,0:T(8,128)(2,1)}, bf16[14,8,640]{2,1,0:T(8,128)(2,1)S(1)}, u32[]{:S(2)}, u32[]{:S(2)}) collective-permute-start(bf16[14,8,640]{2,1,0:T(8,128)(2,1)} %get-tuple-element.802), channel_id=1, source_target_pairs={{32,0},{64,32},{96,64},{128,96},{160,128},{192,160},{224,192},{33,... | collective-permute-start | bytes 430088 | tf_op jit(solution)/shard_map/while/body/eval_jaxpr/ppermute | solution.py:18
  450.0 26.6 %collective-permute-start.4 = (bf16[14,8,640]{2,1,0:T(8,128)(2,1)}, bf16[14,8,640]{2,1,0:T(8,128)(2,1)S(1)}, u32[]{:S(2)}, u32[]{:S(2)}) collective-permute-start(bf16[14,8,640]{2,1,0:T(8,128)(2,1)} %get-tuple-element.802), channel_id=1, source_target_pairs={{32,0},{64,32},{96,64},{128,96},{160,128},{192,160},{224,192},{33,... | collective-permute-start | bytes 430088 | tf_op jit(solution)/shard_map/while/body/eval_jaxpr/ppermute | solution.py:18
  451.9 12.6 %collective-permute-start.5 = (bf16[14,8,640]{2,1,0:T(8,128)(2,1)}, bf16[14,8,640]{2,1,0:T(8,128)(2,1)}, u32[]{:S(2)}, u32[]{:S(2)}) collective-permute-start(bf16[14,8,640]{2,1,0:T(8,128)(2,1)} %get-tuple-element.803), channel_id=1, source_target_pairs={{0,32},{32,0},{64,96},{96,64},{128,160},{160,128},{192,224},{224,1... | collective-permute-start | bytes 430088 | tf_op jit(solution)/shard_map/while/body/eval_jaxpr/ppermute | solution.py:12
  488.1 26.6 %collective-permute-start.4 = (bf16[14,8,640]{2,1,0:T(8,128)(2,1)}, bf16[14,8,640]{2,1,0:T(8,128)(2,1)S(1)}, u32[]{:S(2)}, u32[]{:S(2)}) collective-permute-start(bf16[14,8,640]{2,1,0:T(8,128)(2,1)} %get-tuple-element.802), channel_id=1, source_target_pairs={{32,0},{64,32},{96,64},{128,96},{160,128},{192,160},{224,192},{33,... | collective-permute-start | bytes 430088 | tf_op jit(solution)/shard_map/while/body/eval_jaxpr/ppermute | solution.py:18
  490.0 12.6 %collective-permute-start.5 = (bf16[14,8,640]{2,1,0:T(8,128)(2,1)}, bf16[14,8,640]{2,1,0:T(8,128)(2,1)}, u32[]{:S(2)}, u32[]{:S(2)}) collective-permute-start(bf16[14,8,640]{2,1,0:T(8,128)(2,1)} %get-tuple-element.803), channel_id=1, source_target_pairs={{0,32},{32,0},{64,96},{96,64},{128,160},{160,128},{192,224},{224,1... | collective-permute-start | bytes 430088 | tf_op jit(solution)/shard_map/while/body/eval_jaxpr/ppermute | solution.py:12
  526.1 26.6 %collective-permute-start.4 = (bf16[14,8,640]{2,1,0:T(8,128)(2,1)}, bf16[14,8,640]{2,1,0:T(8,128)(2,1)S(1)}, u32[]{:S(2)}, u32[]{:S(2)}) collective-permute-start(bf16[14,8,640]{2,1,0:T(8,128)(2,1)} %get-tuple-element.802), channel_id=1, source_target_pairs={{32,0},{64,32},{96,64},{128,96},{160,128},{192,160},{224,192},{33,... | collective-permute-start | bytes 430088 | tf_op jit(solution)/shard_map/while/body/eval_jaxpr/ppermute | solution.py:18
  528.0 12.6 %collective-permute-start.5 = (bf16[14,8,640]{2,1,0:T(8,128)(2,1)}, bf16[14,8,640]{2,1,0:T(8,128)(2,1)}, u32[]{:S(2)}, u32[]{:S(2)}) collective-permute-start(bf16[14,8,640]{2,1,0:T(8,128)(2,1)} %get-tuple-element.803), channel_id=1, source_target_pairs={{0,32},{32,0},{64,96},{96,64},{128,160},{160,128},{192,224},{224,1... | collective-permute-start | bytes 430088 | tf_op jit(solution)/shard_map/while/body/eval_jaxpr/ppermute | solution.py:12
  564.2 26.6 %collective-permute-start.4 = (bf16[14,8,640]{2,1,0:T(8,128)(2,1)}, bf16[14,8,640]{2,1,0:T(8,128)(2,1)S(1)}, u32[]{:S(2)}, u32[]{:S(2)}) collective-permute-start(bf16[14,8,640]{2,1,0:T(8,128)(2,1)} %get-tuple-element.802), channel_id=1, source_target_pairs={{32,0},{64,32},{96,64},{128,96},{160,128},{192,160},{224,192},{33,... | collective-permute-start | bytes 430088 | tf_op jit(solution)/shard_map/while/body/eval_jaxpr/ppermute | solution.py:18
  566.1 12.6 %collective-permute-start.5 = (bf16[14,8,640]{2,1,0:T(8,128)(2,1)}, bf16[14,8,640]{2,1,0:T(8,128)(2,1)}, u32[]{:S(2)}, u32[]{:S(2)}) collective-permute-start(bf16[14,8,640]{2,1,0:T(8,128)(2,1)} %get-tuple-element.803), channel_id=1, source_target_pairs={{0,32},{32,0},{64,96},{96,64},{128,160},{160,128},{192,224},{224,1... | collective-permute-start | bytes 430088 | tf_op jit(solution)/shard_map/while/body/eval_jaxpr/ppermute | solution.py:12
  602.3 26.6 %collective-permute-start.4 = (bf16[14,8,640]{2,1,0:T(8,128)(2,1)}, bf16[14,8,640]{2,1,0:T(8,128)(2,1)S(1)}, u32[]{:S(2)}, u32[]{:S(2)}) collective-permute-start(bf16[14,8,640]{2,1,0:T(8,128)(2,1)} %get-tuple-element.802), channel_id=1, source_target_pairs={{32,0},{64,32},{96,64},{128,96},{160,128},{192,160},{224,192},{33,... | collective-permute-start | bytes 430088 | tf_op jit(solution)/shard_map/while/body/eval_jaxpr/ppermute | solution.py:18
  604.2 12.6 %collective-permute-start.5 = (bf16[14,8,640]{2,1,0:T(8,128)(2,1)}, bf16[14,8,640]{2,1,0:T(8,128)(2,1)}, u32[]{:S(2)}, u32[]{:S(2)}) collective-permute-start(bf16[14,8,640]{2,1,0:T(8,128)(2,1)} %get-tuple-element.803), channel_id=1, source_target_pairs={{0,32},{32,0},{64,96},{96,64},{128,160},{160,128},{192,224},{224,1... | collective-permute-start | bytes 430088 | tf_op jit(solution)/shard_map/while/body/eval_jaxpr/ppermute | solution.py:12
  (143 other events, 951.7 us)
Sparse Core Ops, SparseCore 0:
  629.0 247.1 all-reduce.8
where the time goes:
time: 895 us; the launch traced here: 891 us
  waiting for transfers between devices  354 us (40%)
  matrix products  148 us (17%)
  starting transfers between devices  126 us (14%)
  local copies, waits for them, and re-layouts  92.9 us (10%)
  other arithmetic  76.6 us (9%)
  blocking collectives  53.6 us (6%)
  loops' own time  26.4 us (3%)
  between operations  14.2 us (2%)
    psum x1, waiting for transfers between devices, local(): lax.psum((total_skip, total_conv, total_gain), 'dp')  193 us
    ppermute x54, waiting for transfers between devices, swapped(): return lax.ppermute(value, axis, pairs)  161 us
    dot_general x18, matrix products, outer_sum(): lax.dot_general(left, right, (((0, 1), (0, 1)), ((), ())), preferred_elem...  74.7 us
    ppermute x54, starting transfers between devices, swapped(): return lax.ppermute(value, axis, pairs)  70.8 us
    ppermute x18, starting transfers between devices, passed_along(): lax.ppermute(value, axis, [(source, source + steps) for source in range(i...  55 us
    psum x1, blocking collectives, local(): lax.psum((total_skip, total_conv, total_gain), 'dp')  53.6 us
    dot_general x18, matrix products, right_dot(): lax.dot_general(left, right, (((2,), (0,)), ((), ())), preferred_element_...  38.9 us
    dot_general x18, matrix products, right_dot_transposed(): lax.dot_general(left, right, (((2,), (1,)), ((), ())), preferred_element_...  32.4 us
  transfers between devices with their start and end apart: 73, of which 46 were waited for; matrix products, arithmetic and copies ran while one was open for 16% of the time, Pallas kernels for 0%

commit v1 on v0

v1 whole, which is shorter than its diff:
```python
import jax
import jax.numpy as jnp
from jax import lax
from jax.experimental import pallas as pl
from jax.experimental.pallas import tpu as pltpu
from jax.sharding import PartitionSpec as P

EPSILON = 1e-05
LOW = jnp.bfloat16
HIGH = jnp.float32
VMEM_BYTES = 24 * 2**20


def dot(left, right):
    return lax.dot_general(left, right, (((1,), (0,)), ((), ())), preferred_element_type=HIGH)


def dot_transposed(left, right):
    return lax.dot_general(left, right, (((1,), (1,)), ((), ())), preferred_element_type=HIGH)


def dot_outer(left, right):
    return lax.dot_general(left, right, (((0,), (0,)), ((), ())), preferred_element_type=HIGH)


def later(value, pixels):
    return jnp.concatenate([jnp.zeros_like(value[:pixels]), value[:-pixels]], axis=0)


def earlier(value, pixels):
    return jnp.concatenate([value[pixels:], jnp.zeros_like(value[:pixels])], axis=0)


def level_forward(x, s, skip_ref, conv_ref, gain, embed, pixels):
    width = skip_ref.shape[0]
    mixed = x.astype(HIGH) + dot(s, skip_ref[...]) + embed
    inv_rms = lax.rsqrt(jnp.mean(mixed * mixed, axis=-1, keepdims=True) + EPSILON)
    unit = mixed * inv_rms
    normed = (unit * gain).astype(LOW)
    before = dot(normed, conv_ref[:width])
    middle = dot(normed, conv_ref[width : 2 * width])
    after = dot(normed, conv_ref[2 * width :])
    conv_out = middle + later(before, pixels) + earlier(after, pixels)
    return mixed, inv_rms, unit, normed, conv_out


def forward_kernel(pixels, same, *refs):
    if same:
        x_ref, skip_ref, conv_ref, gain_ref, embed_ref, out_ref = refs
        x = x_ref[...]
        s = x
    else:
        x_ref, s_ref, skip_ref, conv_ref, gain_ref, embed_ref, out_ref = refs
        x = x_ref[...]
        s = s_ref[...]
    mixed, _, _, _, conv_out = level_forward(
        x, s, skip_ref, conv_ref, gain_ref[...], embed_ref[...], pixels
    )
    out_ref[...] = (mixed + conv_out * jax.nn.sigmoid(conv_out)).astype(LOW)


def saved_kernel(pixels, x_ref, s_ref, skip_ref, conv_ref, gain_ref, embed_ref,
                 inv_ref, unit_ref, normed_ref, slope_ref):
    _, inv_rms, unit, normed, conv_out = level_forward(
        x_ref[...], s_ref[...], skip_ref, conv_ref, gain_ref[...], embed_ref[...], pixels
    )
    sigmoid = jax.nn.sigmoid(conv_out)
    inv_ref[...] = jnp.broadcast_to(inv_rms, inv_ref.shape)
    unit_ref[...] = unit
    normed_ref[...] = normed
    slope_ref[...] = sigmoid * (1.0 + conv_out * (1.0 - sigmoid))


def level_backward(d, slope, unit, inv_rms, conv_ref, gain, pixels):
    width = conv_ref.shape[1]
    conv_grad = d * slope
    conv_low = conv_grad.astype(LOW)
    first = dot_transposed(conv_low, conv_ref[:width])
    middle = dot_transposed(conv_low, conv_ref[width : 2 * width])
    last = dot_transposed(conv_low, conv_ref[2 * width :])
    normed_grad = middle + earlier(first, pixels) + later(last, pixels)
    scaled = normed_grad * gain
    mixed_grad = d + inv_rms * (
        scaled - unit * jnp.mean(scaled * unit, axis=-1, keepdims=True)
    )
    return conv_grad, normed_grad, mixed_grad


def backward_kernel(pixels, joined, with_skip, *refs):
    if with_skip:
        d_ref, extra_ref, *refs = refs
        d = d_ref[...].astype(HIGH) + extra_ref[...].astype(HIGH)
    else:
        d_ref, *refs = refs
        d = d_ref[...].astype(HIGH)
    inv_ref, unit_ref, slope_ref, skip_ref, conv_ref, gain_ref, *outs = refs
    _, _, mixed_grad = level_backward(
        d, slope_ref[...], unit_ref[...], inv_ref[:, :1], conv_ref, gain_ref[...], pixels
    )
    skip_grad = dot_transposed(mixed_grad.astype(LOW), skip_ref[...])
    if joined:
        outs[0][...] = (mixed_grad + skip_grad).astype(LOW)
    else:
        outs[0][...] = mixed_grad.astype(LOW)
        outs[1][...] = skip_grad.astype(LOW)


def last_kernel(pixels, clips, *refs):
    d_refs, refs = refs[:clips], refs[clips:]
    e_refs, refs = refs[:clips], refs[clips:]
    inv_refs, refs = refs[:clips], refs[clips:]
    unit_refs, refs = refs[:clips], refs[clips:]
    slope_refs, refs = refs[:clips], refs[clips:]
    normed_refs, refs = refs[:clips], refs[clips:]
    s_refs, refs = refs[:clips], refs[clips:]
    conv_ref, gain_ref, grad_ref, gain_out_ref = refs
    width = conv_ref.shape[1]
    gain_total = jnp.zeros((1, width), HIGH)
    shifted = ([], [], [])
    mixed_lows = []
    for c in range(clips):
        d = d_refs[c][...].astype(HIGH) + e_refs[c][...].astype(HIGH)
        unit = unit_refs[c][...]
        conv_grad, normed_grad, mixed_grad = level_backward(
            d, slope_refs[c][...], unit, inv_refs[c][:, :1], conv_ref, gain_ref[...], pixels
        )
        gain_total = gain_total + jnp.sum(normed_grad * unit, axis=0, keepdims=True)
        shifted[0].append(earlier(conv_grad, pixels).astype(LOW))
        shifted[1].append(conv_grad.astype(LOW))
        shifted[2].append(later(conv_grad, pixels).astype(LOW))
        mixed_lows.append(mixed_grad.astype(LOW))
    normed = jnp.concatenate([r[...] for r in normed_refs], axis=0)
    s = jnp.concatenate([r[...] for r in s_refs], axis=0)
    grad_ref[:width] = dot_outer(s, jnp.concatenate(mixed_lows, axis=0)).astype(LOW)
    for tap in range(3):
        grad_ref[(tap + 1) * width : (tap + 2) * width] = dot_outer(
            normed, jnp.concatenate(shifted[tap], axis=0)
        ).astype(LOW)
    gain_out_ref[...] = gain_total


def call(kernel, name, outs, *args):
    single = not isinstance(outs, tuple)
    return pl.pallas_call(
        kernel,
        out_shape=outs,
        name=name,
        compiler_params=pltpu.CompilerParams(vmem_limit_bytes=VMEM_BYTES),
    )(*args)


def make_local(sizes):
    sections = sizes["section"]
    dp = sizes["dp"]
    half = sections // 2
    cross = 2
    ring = dp // 4

    def local(clips, cotangent, timesteps, time_table, skip_weights, conv_weights, gains):
        both = ("section", "dp")
        section = lax.axis_index("section")
        member = lax.axis_index("dp")
        core = member % 2
        z = member // 4
        count, frames, pixels, width = clips.shape
        rows = frames * pixels
        skip_weight = skip_weights[0]
        conv_weight = conv_weights[0]
        gain = gains
        low_rows = jax.ShapeDtypeStruct((rows, width), LOW)
        high_rows = jax.ShapeDtypeStruct((rows, width), HIGH)

        def send(value, source, target):
            flip = cross if (source - target) % 2 else 0
            return lax.ppermute(
                value, both, [(source * dp + i, target * dp + (i ^ flip)) for i in range(dp)]
            )

        def within(value, move, only=range(sections)):
            return lax.ppermute(
                value, both, [(s * dp + i, s * dp + move(i)) for s in only for i in range(dp)]
            )

        odd = section % 2 == 1
        swapped_steps = within(timesteps, lambda i: i ^ cross, range(1, sections, 2))
        steps = jnp.where(odd, swapped_steps, timesteps)
        embeds = jnp.take(time_table[0], steps, axis=0).astype(HIGH)
        embed = [embeds[m : m + 1] for m in range(count)]
        first_clips = [clips[m].reshape(rows, width) for m in range(count)]
        last_cotangent = cotangent.reshape(count, rows, width)
        last_section = sections - 1
        if last_section % 2:
            last_cotangent = within(last_cotangent, lambda i: i ^ cross, [last_section])
        zero = jnp.zeros((rows, width), LOW)

        received = [[None] * sections for _ in range(count)]
        skips = [[None] * sections for _ in range(count)]
        for m in range(count):
            received[m][0] = first_clips[m]
        for t in range(sections - 1):
            for m in range(count):
                x = received[m][t]
                if t <= half:
                    out = call(
                        lambda *r: forward_kernel(pixels, True, *r), "fwd", low_rows,
                        x, skip_weight, conv_weight, gain, embed[m],
                    )
                else:
                    out = call(
                        lambda *r: forward_kernel(pixels, False, *r), "fwd_skip", low_rows,
                        x, skips[m][t], skip_weight, conv_weight, gain, embed[m],
                    )
                received[m][t + 1] = send(out, t, t + 1)
                if t < half - 1:
                    out, _ = lax.optimization_barrier((out, received[m][t + 1]))
                    skips[m][last_section - t] = send(out, t, last_section - t)

        is_first = section == 0
        saved = []
        for m in range(count):
            x = jnp.where(is_first, first_clips[m], zero)
            for t in range(1, sections):
                x = x + received[m][t]
            s = jnp.where(section > half, zero, x)
            for t in range(half + 1, sections):
                s = s + skips[m][t]
            inv, unit, normed, slope = call(
                lambda *r: saved_kernel(pixels, *r), "saved",
                (jax.ShapeDtypeStruct((rows, 128), HIGH), high_rows, low_rows, high_rows),
                x, s, skip_weight, conv_weight, gain, embed[m],
            )
            saved.append((inv, unit, normed, slope, s))

        is_last = section == last_section
        grads = [[None] * sections for _ in range(count)]
        extras = [[None] * half for _ in range(count)]
        for m in range(count):
            grads[m][last_section] = last_cotangent[m]
        for t in range(last_section, 0, -1):
            for m in range(count):
                inv, unit, normed, slope, s = saved[m]
                joined = t <= half
                with_skip = t < half - 1
                args = (grads[m][t],) + ((extras[m][t],) if with_skip else ())
                result = call(
                    lambda *r, joined=joined, with_skip=with_skip: backward_kernel(
                        pixels, joined, with_skip, *r
                    ),
                    "bwd",
                    low_rows if joined else (low_rows, low_rows),
                    *args, inv, unit, slope, skip_weight, conv_weight, gain,
                )
                if joined:
                    grads[m][t - 1] = send(result, t, t - 1)
                else:
                    grads[m][t - 1] = send(result[0], t, t - 1)
                    side, _ = lax.optimization_barrier((result[1], grads[m][t - 1]))
                    extras[m][last_section - t] = send(side, t, last_section - t)

        d_parts = []
        e_parts = []
        for m in range(count):
            e = jnp.where(is_last, last_cotangent[m], zero)
            for t in range(sections - 2, 0, -1):
                e = e + grads[m][t]
            for t in range(half - 1):
                e = e + extras[m][t]
            e_parts.append(e)
            d_parts.append(grads[m][0])
        flat = lambda k: [saved[m][k] for m in range(count)]
        taps = 4
        grad, gain_part = call(
            lambda *r: last_kernel(pixels, count, *r), "last",
            (jax.ShapeDtypeStruct((taps * width, width), LOW), jax.ShapeDtypeStruct((1, width), HIGH)),
            *d_parts, *e_parts, *flat(0), *flat(1), *flat(3), *flat(2), *flat(4),
            conv_weight, gain,
        )
        return finish(grad, gain_part, within, member, core, z, width, count * dp)

    def finish(grad, gain_part, within, member, core, z, width, total):
        summed = lax.psum(grad, "dp").astype(HIGH)
        gain_sum = lax.psum(gain_part, "dp")
        return (
            (summed[:width] / total)[None],
            (summed[width:] / total)[None],
            gain_sum / total,
        )

    return local


def solution(mesh):
    placed = (
        P("dp", None, None, None),
        P("dp", None, None, None),
        P("dp"),
        P("section", None, None),
        P("section", None, None),
        P("section", None, None),
        P("section", None),
    )
    return jax.shard_map(
        make_local(dict(mesh.shape)),
        mesh=mesh,
        in_specs=placed,
        out_specs=(P("section", None, None), P("section", None, None), P("section", None)),
        check_vma=False,
    )
```

time: 895 us -> 465 us (0.52)
  matrix products: 148 us -> 0 us
  waiting for transfers between devices: 354 us -> 208 us
  local copies, waits for them, and re-layouts: 92.9 us -> 14.8 us
  other arithmetic: 76.6 us -> 12.1 us
  Pallas kernels: 0 us -> 47.7 us
  loops' own time: 26.4 us -> 0 us
  starting transfers between devices: 126 us -> 107 us
    dot_general x55 -> x0, matrix products: 148 us -> none  [the longest x18 74.7 us: outer_sum(): lax.dot_general(left, right, (((0, 1), (0, 1)), ((), ())), preferred_elem...]
    ppermute x72 -> x42, waiting for transfers between devices: 161 us -> 27.8 us  [the longest x40 27.8 us: send(): lax.ppermute(value, both, [(source * dp + i, target * dp + (i ^ flip)) fo...]
    dynamic_slice x90 -> x0, local copies, waits for them, and re-layouts: 67.3 us -> none  [the longest x36 25.9 us: store(): kept = lax.dynamic_index_in_dim(buffer, slot_safe, 0, keepdims=False)]
    pallas_call x0 -> x31, Pallas kernels: none -> 47.7 us  [call(): pl.pallas_call(kernel, out_shape=outs, name=name, compiler_params=pltpu.C...]
    dynamic_update_slice x36 -> x0, other arithmetic: 30.1 us -> none  [store(): lax.dynamic_update_index_in_dim(buffer, jnp.where(active, value, kept), s...]
    another operation x2 -> x0, loops' own time: 26.4 us -> none  [the longest x1 14.4 us: local(): lax.scan(backward_tick, backward_state, jnp.arange(tick_count, dtype=jnp....]
    convert_element_type x18 -> x2, other arithmetic: 21.8 us -> 2.43 us  [the longest x1 2.35 us: finish(): summed = lax.psum(grad, 'dp').astype(HIGH)]
    ppermute x72 -> x42, starting transfers between devices: 126 us -> 107 us  [the longest x40 77.5 us: send(): lax.ppermute(value, both, [(source * dp + i, target * dp + (i ^ flip)) fo...]
  transfers between devices with their start and end apart: 73 -> 43, of which waited for: 46 -> 6; matrix products, arithmetic and copies ran while one was open for 16% -> 2% of each run, Pallas kernels for 0% -> 9%
where the time goes in v1:
time: 465 us; the launch traced here: 464 us
  waiting for transfers between devices  208 us (45%)
  starting transfers between devices  107 us (23%)
  blocking collectives  58.4 us (13%)
  Pallas kernels  47.7 us (10%)
  between operations  15.3 us (3%)
  local copies, waits for them, and re-layouts  14.8 us (3%)
  other arithmetic  12.1 us (3%)
    psum x1, waiting for transfers between devices, finish(): summed = lax.psum(grad, 'dp').astype(HIGH)  180 us
    ppermute x40, starting transfers between devices, send(): lax.ppermute(value, both, [(source * dp + i, target * dp + (i ^ flip)) fo...  77.5 us
    psum x1, blocking collectives, finish(): gain_sum = lax.psum(gain_part, 'dp')  58.4 us
    pallas_call x31, Pallas kernels, call(): pl.pallas_call(kernel, out_shape=outs, name=name, compiler_params=pltpu.C...  47.7 us
    ppermute x2, starting transfers between devices, within(): lax.ppermute(value, both, [(s * dp + i, s * dp + move(i)) for s in only f...  30 us
    ppermute x40, waiting for transfers between devices, send(): lax.ppermute(value, both, [(source * dp + i, target * dp + (i ^ flip)) fo...  27.8 us
    unnamed x106, local copies, waits for them, and re-layouts  12.2 us
  transfers between devices with their start and end apart: 43, of which 6 were waited for; matrix products, arithmetic and copies ran while one was open for 2% of the time, Pallas kernels for 9%

profile of v1, /device:TPU:8, one launch (start us, length us, event | category | flops | bytes accessed | tf_op | source)
XLA Modules:
  0.0 464.0 jit_solution(4487443299191774825)
XLA Ops:
  7.2 13.5 %collective-permute-start.1 = (s32[2]{0:T(128)}, s32[2]{0:T(128)S(1)}, u32[]{:S(2)}, u32[]{:S(2)}) collective-permute-start(s32[2]{0:T(128)} %param.9), channel_id=1, source_target_pairs={{32,34},{33,35},{34,32},{35,33},{36,38},{37,39},{38,36},{39,37},{4... | collective-permute-start | bytes 32 | tf_op jit(solution)/shard_map/ppermute | solution.py:180
  35.4 13.0 %collective-permute-done.22.r_0_ = bf16[112,640]{1,0:T(8,128)(2,1)S(1)} collective-permute-done((bf16[112,640]{1,0:T(8,128)(2,1)}, bf16[112,640]{1,0:T(8,128)(2,1)S(1)}, u32[]{:S(2)}, u32[]{:S(2)}) %collective-permute-start.22) | collective-permute-done | bytes 143392 | tf_op jit(solution)/shard_map/ppermute | solution.py:175
  61.3 16.5 %collective-permute-start = (bf16[2,112,640]{2,1,0:T(8,128)(2,1)}, bf16[2,112,640]{2,1,0:T(8,128)(2,1)}, u32[]{:S(2)}, u32[]{:S(2)}) collective-permute-start(bf16[2,112,640]{2,1,0:T(8,128)(2,1)} %bitcast), channel_id=1, source_target_pairs={{224,226},{225,227},{226,224},{227,225},{228,230},{229,231},{230,2... | collective-permute-start | bytes 860168 | tf_op jit(solution)/shard_map/ppermute | solution.py:180
  77.7 5.5 %collective-permute-start.7 = (bf16[112,640]{1,0:T(8,128)(2,1)}, bf16[112,640]{1,0:T(8,128)(2,1)S(1)}, u32[]{:S(2)}, u32[]{:S(2)}) collective-permute-start(bf16[112,640]{1,0:T(8,128)(2,1)} %fwd.12), channel_id=1, source_target_pairs={{64,162},{65,163},{66,160},{67,161},{68,166},{69,167},{70,164},{71... | collective-permute-start | bytes 430088 | tf_op jit(solution)/shard_map/ppermute | solution.py:175
  97.2 2.0 fwd_skip.7
  105.4 2.0 bwd.21
  107.5 13.8 %collective-permute-start.31 = (bf16[112,640]{1,0:T(8,128)(2,1)S(1)}, bf16[112,640]{1,0:T(8,128)(2,1)S(1)}, u32[]{:S(2)}, u32[]{:S(2)}) collective-permute-start(bf16[112,640]{1,0:T(8,128)(2,1)S(1)} %get-tuple-element.56), channel_id=1, source_target_pairs={{224,194},{225,195},{226,192},{227,193},{228,198},{229,199},{230,1... | collective-permute-start | bytes 430088 | tf_op jit(solution)/shard_map/ppermute | solution.py:175
  126.7 12.9 %collective-permute-start.12 = (bf16[112,640]{1,0:T(8,128)(2,1)S(1)}, bf16[112,640]{1,0:T(8,128)(2,1)S(1)}, u32[]{:S(2)}, u32[]{:S(2)}) collective-permute-start(bf16[112,640]{1,0:T(8,128)(2,1)S(1)} %get-tuple-element.43), channel_id=1, source_target_pairs={{224,194},{225,195},{226,192},{227,193},{228,198},{229,199},{230,1... | collective-permute-start | bytes 430088 | tf_op jit(solution)/shard_map/ppermute | solution.py:175
  139.6 2.1 bwd.22
  142.4 2.0 bwd.15
  163.4 6.9 %collective-permute-done.36.r_1_ = bf16[112,640]{1,0:T(8,128)(2,1)S(1)} collective-permute-done((bf16[112,640]{1,0:T(8,128)(2,1)S(1)}, bf16[112,640]{1,0:T(8,128)(2,1)S(1)}, u32[]{:S(2)}, u32[]{:S(2)}) %collective-permute-start.36) | collective-permute-done | bytes 143392 | tf_op jit(solution)/shard_map/ppermute | solution.py:175
  171.5 6.6 %collective-permute-done.35.r_0_ = bf16[112,640]{1,0:T(8,128)(2,1)S(1)} collective-permute-done((bf16[112,640]{1,0:T(8,128)(2,1)S(1)}, bf16[112,640]{1,0:T(8,128)(2,1)S(1)}, u32[]{:S(2)}, u32[]{:S(2)}) %collective-permute-start.35) | collective-permute-done | bytes 143392 | tf_op jit(solution)/shard_map/ppermute | solution.py:175
  178.2 2.0 bwd.26
  180.2 2.0 collective-permute-start.37
  182.1 2.0 bwd.19
  184.1 1.9 collective-permute-start.18
  186.1 9.2 %collective-permute-start.41 = (bf16[112,640]{1,0:T(8,128)(2,1)}, bf16[112,640]{1,0:T(8,128)(2,1)}, u32[]{:S(2)}, u32[]{:S(2)}) collective-permute-start(bf16[112,640]{1,0:T(8,128)(2,1)} %get-tuple-element.66), channel_id=1, source_target_pairs={{224,2},{225,3},{226,0},{227,1},{228,6},{229,7},{230,4},{231,5},{2... | collective-permute-start | bytes 430088 | tf_op jit(solution)/shard_map/ppermute | solution.py:175
  197.7 2.4 bwd.27
  201.0 2.6 bwd.20
  206.9 3.0 last.1
  211.6 58.4 %psum.15 = f32[1,640]{1,0:T(1,128)S(1)} all-reduce(f32[1,640]{1,0:T(1,128)S(1)} %get-tuple-element.70), channel_id=1, replica_groups=mesh['section'=8,'dp'=32] {'dp'}, use_global_device_ids=true, to_apply=%region_1.2 | all-reduce | flops 640 | bytes 5120 | tf_op jit(solution)/shard_map/psum | solution.py:282
  270.6 180.4 %all-reduce.2.cloned.1.call-done = bf16[2560,640]{1,0:T(8,128)(2,1)} async-done(((bf16[2560,640]{1,0:T(8,128)(2,1)}), bf16[2560,640]{1,0:T(8,128)(2,1)}) %all-reduce.2.cloned.1.call-update) | async-done | bytes 3276816 | tf_op jit(solution)/shard_map/psum | solution.py:281
  451.0 2.3 convert_element_type.7
  454.6 2.6 fusion
  (216 shorter events, 83.3 us)
Async XLA Ops:
  7.2 443.8 %all-reduce.2.cloned.1.call-start = ((), (), s32[]{:S(2)}) async-start(), calls=%async_computation | async-start | bytes 6553600 | tf_op jit(solution)/shard_map/psum | solution.py:281
  7.2 14.5 %collective-permute-start.1 = (s32[2]{0:T(128)}, s32[2]{0:T(128)S(1)}, u32[]{:S(2)}, u32[]{:S(2)}) collective-permute-start(s32[2]{0:T(128)} %param.9), channel_id=1, source_target_pairs={{32,34},{33,35},{34,32},{35,33},{36,38},{37,39},{38,36},{39,37},{4... | collective-permute-start | bytes 32 | tf_op jit(solution)/shard_map/ppermute | solution.py:180
  31.8 16.6 %collective-permute-start.22 = (bf16[112,640]{1,0:T(8,128)(2,1)}, bf16[112,640]{1,0:T(8,128)(2,1)S(1)}, u32[]{:S(2)}, u32[]{:S(2)}) collective-permute-start(bf16[112,640]{1,0:T(8,128)(2,1)} %fwd.16), channel_id=1, source_target_pairs={{32,66},{33,67},{34,64},{35,65},{36,70},{37,71},{38,68},{39,69},{4... | collective-permute-start | bytes 430088 | tf_op jit(solution)/shard_map/ppermute | solution.py:175
  34.1 16.6 %collective-permute-start.3 = (bf16[112,640]{1,0:T(8,128)(2,1)S(1)}, bf16[112,640]{1,0:T(8,128)(2,1)S(1)}, u32[]{:S(2)}, u32[]{:S(2)}) collective-permute-start(bf16[112,640]{1,0:T(8,128)(2,1)S(1)} %fwd.11), channel_id=1, source_target_pairs={{32,66},{33,67},{34,64},{35,65},{36,70},{37,71},{38,68},{39,69},{4... | collective-permute-start | bytes 430088 | tf_op jit(solution)/shard_map/ppermute | solution.py:175
  57.6 25.7 %collective-permute-start.5 = (bf16[112,640]{1,0:T(8,128)(2,1)S(1)}, bf16[112,640]{1,0:T(8,128)(2,1)S(1)}, u32[]{:S(2)}, u32[]{:S(2)}) collective-permute-start(bf16[112,640]{1,0:T(8,128)(2,1)S(1)} %fwd.13), channel_id=1, source_target_pairs={{96,130},{97,131},{98,128},{99,129},{100,134},{101,135},{102,132},... | collective-permute-start | bytes 430088 | tf_op jit(solution)/shard_map/ppermute | solution.py:175
  58.3 28.0 %collective-permute-start.26 = (bf16[112,640]{1,0:T(8,128)(2,1)S(1)}, bf16[112,640]{1,0:T(8,128)(2,1)S(1)}, u32[]{:S(2)}, u32[]{:S(2)}) collective-permute-start(bf16[112,640]{1,0:T(8,128)(2,1)S(1)} %fwd.17), channel_id=1, source_target_pairs={{64,162},{65,163},{66,160},{67,161},{68,166},{69,167},{70,164},{71... | collective-permute-start | bytes 430088 | tf_op jit(solution)/shard_map/ppermute | solution.py:175
  60.6 27.0 %collective-permute-start.25 = (bf16[112,640]{1,0:T(8,128)(2,1)S(1)}, bf16[112,640]{1,0:T(8,128)(2,1)S(1)}, u32[]{:S(2)}, u32[]{:S(2)}) collective-permute-start(bf16[112,640]{1,0:T(8,128)(2,1)S(1)} %fwd.19), channel_id=1, source_target_pairs={{128,162},{129,163},{130,160},{131,161},{132,166},{133,167},{134,1... | collective-permute-start | bytes 430088 | tf_op jit(solution)/shard_map/ppermute | solution.py:175
  61.3 38.0 %collective-permute-start = (bf16[2,112,640]{2,1,0:T(8,128)(2,1)}, bf16[2,112,640]{2,1,0:T(8,128)(2,1)}, u32[]{:S(2)}, u32[]{:S(2)}) collective-permute-start(bf16[2,112,640]{2,1,0:T(8,128)(2,1)} %bitcast), channel_id=1, source_target_pairs={{224,226},{225,227},{226,224},{227,225},{228,230},{229,231},{230,2... | collective-permute-start | bytes 860168 | tf_op jit(solution)/shard_map/ppermute | solution.py:180
  77.7 12.8 %collective-permute-start.7 = (bf16[112,640]{1,0:T(8,128)(2,1)}, bf16[112,640]{1,0:T(8,128)(2,1)S(1)}, u32[]{:S(2)}, u32[]{:S(2)}) collective-permute-start(bf16[112,640]{1,0:T(8,128)(2,1)} %fwd.12), channel_id=1, source_target_pairs={{64,162},{65,163},{66,160},{67,161},{68,166},{69,167},{70,164},{71... | collective-permute-start | bytes 430088 | tf_op jit(solution)/shard_map/ppermute | solution.py:175
  90.6 30.7 %collective-permute-start.11 = (bf16[112,640]{1,0:T(8,128)(2,1)S(1)}, bf16[112,640]{1,0:T(8,128)(2,1)S(1)}, u32[]{:S(2)}, u32[]{:S(2)}) collective-permute-start(bf16[112,640]{1,0:T(8,128)(2,1)S(1)} %fwd.10), channel_id=1, source_target_pairs={{0,226},{1,227},{2,224},{3,225},{4,230},{5,231},{6,228},{7,229},{8... | collective-permute-start | bytes 430088 | tf_op jit(solution)/shard_map/ppermute | solution.py:175
  91.2 11.4 %collective-permute-start.30 = (bf16[112,640]{1,0:T(8,128)(2,1)}, bf16[112,640]{1,0:T(8,128)(2,1)S(1)}, u32[]{:S(2)}, u32[]{:S(2)}) collective-permute-start(bf16[112,640]{1,0:T(8,128)(2,1)} %copy-done.49), channel_id=1, source_target_pairs={{0,226},{1,227},{2,224},{3,225},{4,230},{5,231},{6,228},{7,229},{8... | collective-permute-start | bytes 430088 | tf_op jit(solution)/shard_map/ppermute | solution.py:175
  101.9 19.4 %collective-permute-start.10 = (bf16[112,640]{1,0:T(8,128)(2,1)S(1)}, bf16[112,640]{1,0:T(8,128)(2,1)S(1)}, u32[]{:S(2)}, u32[]{:S(2)}) collective-permute-start(bf16[112,640]{1,0:T(8,128)(2,1)S(1)} %fwd_skip.5), channel_id=1, source_target_pairs={{192,226},{193,227},{194,224},{195,225},{196,230},{197,231},{198,2... | collective-permute-start | bytes 430088 | tf_op jit(solution)/shard_map/ppermute | solution.py:175
  107.5 32.1 %collective-permute-start.31 = (bf16[112,640]{1,0:T(8,128)(2,1)S(1)}, bf16[112,640]{1,0:T(8,128)(2,1)S(1)}, u32[]{:S(2)}, u32[]{:S(2)}) collective-permute-start(bf16[112,640]{1,0:T(8,128)(2,1)S(1)} %get-tuple-element.56), channel_id=1, source_target_pairs={{224,194},{225,195},{226,192},{227,193},{228,198},{229,199},{230,1... | collective-permute-start | bytes 430088 | tf_op jit(solution)/shard_map/ppermute | solution.py:175
  126.7 15.6 %collective-permute-start.12 = (bf16[112,640]{1,0:T(8,128)(2,1)S(1)}, bf16[112,640]{1,0:T(8,128)(2,1)S(1)}, u32[]{:S(2)}, u32[]{:S(2)}) collective-permute-start(bf16[112,640]{1,0:T(8,128)(2,1)S(1)} %get-tuple-element.43), channel_id=1, source_target_pairs={{224,194},{225,195},{226,192},{227,193},{228,198},{229,199},{230,1... | collective-permute-start | bytes 430088 | tf_op jit(solution)/shard_map/ppermute | solution.py:175
  153.3 16.9 %collective-permute-start.36 = (bf16[112,640]{1,0:T(8,128)(2,1)S(1)}, bf16[112,640]{1,0:T(8,128)(2,1)S(1)}, u32[]{:S(2)}, u32[]{:S(2)}) collective-permute-start(bf16[112,640]{1,0:T(8,128)(2,1)S(1)} %get-tuple-element.60), channel_id=1, source_target_pairs={{160,66},{161,67},{162,64},{163,65},{164,70},{165,71},{166,68},{16... | collective-permute-start | bytes 430088 | tf_op jit(solution)/shard_map/ppermute | solution.py:175
  156.8 21.3 %collective-permute-start.35 = (bf16[112,640]{1,0:T(8,128)(2,1)S(1)}, bf16[112,640]{1,0:T(8,128)(2,1)S(1)}, u32[]{:S(2)}, u32[]{:S(2)}) collective-permute-start(bf16[112,640]{1,0:T(8,128)(2,1)S(1)} %bwd.25), channel_id=1, source_target_pairs={{96,66},{97,67},{98,64},{99,65},{100,70},{101,71},{102,68},{103,69... | collective-permute-start | bytes 430088 | tf_op jit(solution)/shard_map/ppermute | solution.py:175
  158.1 24.0 %collective-permute-start.17 = (bf16[112,640]{1,0:T(8,128)(2,1)S(1)}, bf16[112,640]{1,0:T(8,128)(2,1)S(1)}, u32[]{:S(2)}, u32[]{:S(2)}) collective-permute-start(bf16[112,640]{1,0:T(8,128)(2,1)S(1)} %get-tuple-element.47), channel_id=1, source_target_pairs={{160,66},{161,67},{162,64},{163,65},{164,70},{165,71},{166,68},{16... | collective-permute-start | bytes 430088 | tf_op jit(solution)/shard_map/ppermute | solution.py:175
  160.8 21.4 %collective-permute-start.16 = (bf16[112,640]{1,0:T(8,128)(2,1)S(1)}, bf16[112,640]{1,0:T(8,128)(2,1)S(1)}, u32[]{:S(2)}, u32[]{:S(2)}) collective-permute-start(bf16[112,640]{1,0:T(8,128)(2,1)S(1)} %bwd.18), channel_id=1, source_target_pairs={{96,66},{97,67},{98,64},{99,65},{100,70},{101,71},{102,68},{103,69... | collective-permute-start | bytes 430088 | tf_op jit(solution)/shard_map/ppermute | solution.py:175
  162.1 33.2 %collective-permute-start.38 = (bf16[112,640]{1,0:T(8,128)(2,1)}, bf16[112,640]{1,0:T(8,128)(2,1)}, u32[]{:S(2)}, u32[]{:S(2)}) collective-permute-start(bf16[112,640]{1,0:T(8,128)(2,1)} %get-tuple-element.62), channel_id=1, source_target_pairs={{192,34},{193,35},{194,32},{195,33},{196,38},{197,39},{198,36},{19... | collective-permute-start | bytes 430088 | tf_op jit(solution)/shard_map/ppermute | solution.py:175
  170.2 30.7 %collective-permute-start.19 = (bf16[112,640]{1,0:T(8,128)(2,1)}, bf16[112,640]{1,0:T(8,128)(2,1)}, u32[]{:S(2)}, u32[]{:S(2)}) collective-permute-start(bf16[112,640]{1,0:T(8,128)(2,1)} %get-tuple-element.49), channel_id=1, source_target_pairs={{192,34},{193,35},{194,32},{195,33},{196,38},{197,39},{198,36},{19... | collective-permute-start | bytes 430088 | tf_op jit(solution)/shard_map/ppermute | solution.py:175
  180.2 15.8 %collective-permute-start.37 = (bf16[112,640]{1,0:T(8,128)(2,1)}, bf16[112,640]{1,0:T(8,128)(2,1)}, u32[]{:S(2)}, u32[]{:S(2)}) collective-permute-start(bf16[112,640]{1,0:T(8,128)(2,1)} %bwd.26), channel_id=1, source_target_pairs={{64,34},{65,35},{66,32},{67,33},{68,38},{69,39},{70,36},{71,37},{7... | collective-permute-start | bytes 430088 | tf_op jit(solution)/shard_map/ppermute | solution.py:175
  184.1 16.9 %collective-permute-start.18 = (bf16[112,640]{1,0:T(8,128)(2,1)}, bf16[112,640]{1,0:T(8,128)(2,1)}, u32[]{:S(2)}, u32[]{:S(2)}) collective-permute-start(bf16[112,640]{1,0:T(8,128)(2,1)} %bwd.19), channel_id=1, source_target_pairs={{64,34},{65,35},{66,32},{67,33},{68,38},{69,39},{70,36},{71,37},{7... | collective-permute-start | bytes 430088 | tf_op jit(solution)/shard_map/ppermute | solution.py:175
  186.1 18.2 %collective-permute-start.41 = (bf16[112,640]{1,0:T(8,128)(2,1)}, bf16[112,640]{1,0:T(8,128)(2,1)}, u32[]{:S(2)}, u32[]{:S(2)}) collective-permute-start(bf16[112,640]{1,0:T(8,128)(2,1)} %get-tuple-element.66), channel_id=1, source_target_pairs={{224,2},{225,3},{226,0},{227,1},{228,6},{229,7},{230,4},{231,5},{2... | collective-permute-start | bytes 430088 | tf_op jit(solution)/shard_map/ppermute | solution.py:175
  195.3 10.3 %collective-permute-start.40 = (bf16[112,640]{1,0:T(8,128)(2,1)}, bf16[112,640]{1,0:T(8,128)(2,1)S(1)}, u32[]{:S(2)}, u32[]{:S(2)}) collective-permute-start(bf16[112,640]{1,0:T(8,128)(2,1)} %copy-done.51), channel_id=1, source_target_pairs={{224,2},{225,3},{226,0},{227,1},{228,6},{229,7},{230,4},{231,5},{2... | collective-permute-start | bytes 430088 | tf_op jit(solution)/shard_map/ppermute | solution.py:175
  (72 other events, 413.7 us)
Sparse Core Ops, SparseCore 0:
  211.7 239.1 all-reduce.1
